TPU v7x, 32 devices: a whole 2x2x4 slice. The times are simulated.
32 devices in a mesh: section: 2 (over x), img: 4 (over z), ch: 4 (over y, core).
Axes of the slice: x: 2, y: 2, z: 4, core: 2. Of those that a mesh axis runs over, the one named last changes fastest.
Arguments:
- pixels: bfloat16 [8, 32, 28, 640], P('img', 'ch'), may hold values from -6 to 6
- first_gain: float32 [640], replicated, may hold values from 0.25 to 1.75
- first_shift: float32 [640], replicated, may hold values from -3 to 3
- first_kernel: bfloat16 [3, 3, 640, 640], P(None, None, 'img'), may hold values from -0.078125 to 0.078125
- projection: bfloat16 [640, 2560], P('img'), may hold values from -0.25 to 0.25
- second_gain: float32 [2560], replicated, may hold values from 0.25 to 1.75
- second_shift: float32 [2560], replicated, may hold values from -3 to 3
- second_kernel: bfloat16 [3, 3, 2560, 2560], P(None, None, ('img', 'ch')), may hold values from -0.0390625 to 0.0390625
Outputs:
- section_outputs: bfloat16 [2, 8, 16, 14, 2560], P('section', 'img', 'ch')
All inputs are finite; a program needn't handle non-finite values.
Results may differ from a plain program's by a relative error of at most 0.013.
Values may be sent and summed in bfloat16 or wider, within the bound.
No kernel may reach another device: no remote copies, remote signals or barrier semaphores. Data moves between devices by JAX's collectives and lax.ppermute only.
A program may use at most 128 MiB of HBM per device.

v0:
```python
import jax
import jax.numpy as jnp
from jax import lax
from jax.sharding import PartitionSpec as P

LAYOUT = ("NHWC", "HWIO", "NHWC")


def extended(cells, sides, width):
    for axis, dim in sides:
        count = lax.axis_size(axis)
        ends = count - 1
        head = lax.slice_in_dim(cells, 0, width, axis=dim)
        tail = lax.slice_in_dim(cells, cells.shape[dim] - width, cells.shape[dim], axis=dim)
        cells = jnp.concatenate(
            [
                lax.ppermute(tail, axis, [(i, (i + 1) % count) for i in range(ends)]),
                cells,
                lax.ppermute(head, axis, [((i + 1) % count, i) for i in range(ends)]),
            ],
            axis=dim,
        )
    return cells


def from_behind(array, axis, by):
    count = lax.axis_size(axis)
    pairs = [(i, i + by) for i in range(count) if 0 <= i + by < count]
    return lax.ppermute(array, axis, pairs)


def convolve(inputs, kernel, padding):
    return lax.conv_general_dilated(
        inputs,
        kernel,
        (1, 1),
        padding,
        dimension_numbers=LAYOUT,
        preferred_element_type=jnp.float32,
    )


def reduce_resolution(value_entries):
    count, height, breadth, depth = value_entries.shape
    blocks = value_entries.reshape(count, height // 2, 2, breadth // 2, 2, depth)
    return jnp.sum(blocks, axis=(2, 4)) * 0.25


def pick_group(value_entries, groups, shards, member):
    lead = value_entries.shape[:-1]
    per_block = value_entries.shape[-1] // (groups * shards)
    split = value_entries.reshape(lead + (groups, shards, per_block))
    chosen = lax.dynamic_slice_in_dim(split, member, 1, len(lead) + 1)
    return chosen.reshape(lead + (groups * per_block,))


def arrange_groups(value_entries, groups, shards):
    lead = value_entries.shape[:-1]
    per_block = value_entries.shape[-1] // (groups * shards)
    split = value_entries.reshape(lead + (groups, shards, per_block))
    swapped = jnp.swapaxes(split, len(lead), len(lead) + 1)
    return swapped.reshape(lead + (groups * shards * per_block,))


def body(
    pixels,
    first_gain,
    first_shift,
    first_kernel,
    projection,
    second_gain,
    second_shift,
    second_kernel,
):
    section_id = lax.axis_index("section")
    is_first = section_id == 0
    is_second = section_id == 1
    groups = lax.axis_size("img")
    shards = lax.axis_size("ch")
    member = lax.axis_index("ch")
    images, rows, columns, depth = pixels.shape
    out_rows = rows // 2
    out_cols = columns // 2
    wide = second_gain.shape[0]
    normalized_input = jax.nn.relu(pixels.astype(jnp.float32) * first_gain + first_shift).astype(
        jnp.bfloat16
    )
    padded = extended(normalized_input, (("ch", 1),), 1)
    initial_blank = jnp.zeros((images, rows, columns, depth), jnp.float32)
    piece = lax.all_gather(first_kernel, "img", axis=2, tiled=True)

    def first_compute():
        return initial_blank + convolve(padded, piece, ((0, 0), (1, 1)))

    convolved = lax.cond(is_first, first_compute, lambda: initial_blank)
    blended_result = convolved + pixels.astype(jnp.float32)
    averaged_pixels = reduce_resolution(blended_result).astype(jnp.bfloat16)
    all_rows = out_rows * shards
    flat_pooled = averaged_pixels.reshape(images * out_rows * out_cols, depth)

    def project_piece(total, piece):

        def project_compute():
            return jnp.dot(flat_pooled, piece, preferred_element_type=jnp.float32)

        return lax.cond(is_first, project_compute, lambda: total)

    proj_empty = jnp.zeros((flat_pooled.shape[0], wide), jnp.float32)
    summed_proj = project_piece(proj_empty, lax.all_gather(projection, "img", axis=0, tiled=True))
    own_rows = summed_proj.astype(jnp.bfloat16).reshape(images, out_rows, out_cols, wide)
    arrived = from_behind(own_rows, "section", 1)
    sorted_layout = arrange_groups(arrived, groups, shards)
    channel_in = lax.all_to_all(sorted_layout, "ch", split_axis=3, concat_axis=1, tiled=True)
    gain_part = pick_group(second_gain, groups, shards, member)
    shift_part = pick_group(second_shift, groups, shards, member)
    second_in = jax.nn.relu(channel_in.astype(jnp.float32) * gain_part + shift_part).astype(
        jnp.bfloat16
    )

    def second_piece(total, piece):

        def second_compute():
            return total + convolve(second_in, piece, ((1, 1), (1, 1)))

        return lax.cond(is_second, second_compute, lambda: total)

    second_empty = jnp.zeros((images, all_rows, out_cols, wide), jnp.float32)
    partial_value = second_piece(
        second_empty, lax.all_gather(second_kernel, "img", axis=2, tiled=True)
    )
    summed = lax.psum_scatter(
        partial_value.astype(jnp.bfloat16), "ch", scatter_dimension=1, tiled=True
    ).astype(jnp.float32)
    block = (summed + arrived.astype(jnp.float32)).astype(jnp.bfloat16)
    final = jnp.where(is_first, own_rows, block)
    return final[None]


def solution(mesh):
    placed = (
        P("img", "ch", None, None),
        P(),
        P(),
        P(None, None, "img", None),
        P("img", None),
        P(),
        P(),
        P(None, None, ("img", "ch"), None),
    )
    return jax.shard_map(
        body,
        mesh=mesh,
        in_specs=placed,
        out_specs=P("section", "img", "ch", None, None),
        check_vma=False,
    )
```

profile of v0, /device:TPU:0, one launch (start us, length us, event | category | flops | bytes accessed | tf_op | source)
XLA Modules:
  0.0 794.3 jit_solution(10480101129916246538)
XLA Ops:
  9.4 2.4 collective-permute-start
  11.9 1.3 collective-permute-start.1
  13.2 4.1 collective-permute-done.1
  17.9 126.7 %all-gather.4.cloned.1.call-done = bf16[3,3,640,640]{3,2,1,0:T(8,128)(2,1)} async-done(((bf16[3,3,160,640]{3,2,1,0:T(8,128)(2,1)}), bf16[3,3,640,640]{3,2,1,0:T(8,128)(2,1)}) %all-gather.4.cloned.1.call-update) | async-done | bytes 7372816 | tf_op jit(solution)/shard_map/all_gather | solution.py:90
  144.7 10.0 %conditional.3 = (f32[2,8,28,640]{3,1,2,0:T(8,128)S(1)}) conditional(s32[]{:T(128)} %convert_element_type.54, () %tuple.26, (bf16[2,10,28,640]{3,1,2,0:T(8,128)(2,1)S(1)}, bf16[3,3,640,640]{3,2,1,0:T(8,128)(2,1)}) %tuple.27), branch_computations={%region_0.1_spmd, %region_1.2_spmd} | conditional | flops 3778887680 | bytes 21739878 | solution.py:95
  145.9 7.9 convolution_select_fusion
  154.8 0.9 copy.81
  156.4 53.6 %all-gather.6.cloned.1.call-done = bf16[640,2560]{1,0:T(8,128)(2,1)} async-done(((bf16[160,2560]{1,0:T(8,128)(2,1)}), bf16[640,2560]{1,0:T(8,128)(2,1)}) %all-gather.6.cloned.1.call-update) | async-done | bytes 3276816 | tf_op jit(solution)/shard_map/all_gather | solution.py:109
  210.1 3.3 conditional.4
  210.1 2.6 convolution_convert_fusion
  213.4 1.5 collective-permute-start.2
  214.9 12.1 %collective-permute-done.2 = bf16[2,4,14,2560]{3,1,2,0:T(4,128)(2,1)S(1)} collective-permute-done((bf16[2,4,14,2560]{3,1,2,0:T(4,128)(2,1)S(1)}, bf16[2,4,14,2560]{3,1,2,0:T(4,128)(2,1)S(1)}, u32[]{:S(2)}, u32[]{:S(2)}) %collective-permute-start.2) | collective-permute-done | bytes 573472 | tf_op jit(solution)/shard_map/ppermute | solution.py:29
  227.0 1.0 reshape.36
  228.0 5.6 copy.90
  233.7 10.3 %reshape.67 = bf16[4,2,35840]{2,1,0:T(2,128)(2,1)} reshape(bf16[2560,2,4,14]{3,2,1,0:T(4,128)(2,1)} %bitcast.54) | data formatting | bytes 1146880
  244.0 3.5 all-to-all-start
  247.9 8.9 %all-to-all-done = bf16[4,2,35840]{2,1,0:T(2,128)(2,1)S(1)} async-done(((bf16[4,2,35840]{2,1,0:T(2,128)(2,1)}), bf16[4,2,35840]{2,1,0:T(2,128)(2,1)S(1)}, u32[]{:S(2)}, u32[]{:S(2)}) %all-to-all-start) | async-done | bytes 573472 | tf_op jit(solution)/shard_map/all_to_all | solution.py:113
  256.8 12.7 %reshape.68 = bf16[2560,2,4,14]{3,2,1,0:T(4,128)(2,1)} reshape(bf16[4,2,35840]{2,1,0:T(2,128)(2,1)S(1)} %all-to-all-done) | data formatting | bytes 1146880
  269.5 6.8 copy.86
  276.7 0.9 copy.87
  278.4 427.1 %all-gather.8.cloned.1.call-done = bf16[3,3,640,2560]{3,2,1,0:T(8,128)(2,1)} async-done(((bf16[3,3,160,2560]{3,2,1,0:T(8,128)(2,1)}), bf16[3,3,640,2560]{3,2,1,0:T(8,128)(2,1)}) %all-gather.8.cloned.1.call-update) | async-done | bytes 29491216 | tf_op jit(solution)/shard_map/all_gather | solution.py:129
  705.9 1.4 copy-done
  708.6 76.5 %all-reduce.3.cloned.1.call-done = bf16[2,16,14,2560]{3,1,2,0:T(8,128)(2,1)} async-done(((bf16[2,16,14,2560]{3,1,2,0:T(8,128)(2,1)}), bf16[2,16,14,2560]{3,1,2,0:T(8,128)(2,1)}) %all-reduce.3.cloned.1.call-update) | async-done | bytes 2293776
  785.1 2.7 fusion.29
  (55 shorter events, 10.0 us)
Async XLA Ops:
  6.5 138.1 %all-gather.4.cloned.1.call-start = ((), (), s32[]{:S(2)}) async-start(), calls=%async_computation.1 | async-start | bytes 9216000 | tf_op jit(solution)/shard_map/all_gather | solution.py:90
  7.3 202.8 %all-gather.6.cloned.1.call-start = ((), (), s32[]{:S(2)}) async-start(), calls=%async_computation.2 | async-start | bytes 4096000 | tf_op jit(solution)/shard_map/all_gather | solution.py:109
  8.0 1.1 copy-start.1
  8.0 1.1 copy-start.6
  8.0 1.0 copy-start.7
  8.0 697.4 %all-gather.8.cloned.1.call-start = ((), (), s32[]{:S(2)}) async-start(), calls=%async_computation.3 | async-start | bytes 36864000 | tf_op jit(solution)/shard_map/all_gather | solution.py:129
  9.4 3.7 collective-permute-start
  11.9 5.4 collective-permute-start.1
  145.2 0.7 copy-start.9
  213.4 20.3 %copy-start.2 = (bf16[2,4,14,2560]{3,1,2,0:T(4,128)(2,1)}, bf16[2,4,14,2560]{3,1,2,0:T(4,128)(2,1)S(1)}, u32[]{:S(2)}) copy-start(bf16[2,4,14,2560]{3,1,2,0:T(4,128)(2,1)S(1)} %get-tuple-element.60) | copy-start | bytes 1720324
  213.4 13.6 %collective-permute-start.2 = (bf16[2,4,14,2560]{3,1,2,0:T(4,128)(2,1)S(1)}, bf16[2,4,14,2560]{3,1,2,0:T(4,128)(2,1)S(1)}, u32[]{:S(2)}, u32[]{:S(2)}) collective-permute-start(bf16[2,4,14,2560]{3,1,2,0:T(4,128)(2,1)S(1)} %get-tuple-element.60), channel_id=1, source_target_pairs={{0,16},{1,17},{2,18},{3,19},{4,20},{5,21},{6,22},{7,23},{8,24},{9,... | collective-permute-start | bytes 1720328 | tf_op jit(solution)/shard_map/ppermute | solution.py:29
  233.7 13.8 %copy-start.4 = (f32[2560]{0:T(1024)S(1)}, f32[2560]{0:T(1024)}, u32[]{:S(2)}) copy-start(f32[2560]{0:T(1024)} %param.19) | copy-start | bytes 30724
  233.7 13.9 %copy-start.5 = (f32[2560]{0:T(1024)S(1)}, f32[2560]{0:T(1024)}, u32[]{:S(2)}) copy-start(f32[2560]{0:T(1024)} %param.20) | copy-start | bytes 30724
  244.0 12.8 %all-to-all-start = ((bf16[4,2,35840]{2,1,0:T(2,128)(2,1)}), bf16[4,2,35840]{2,1,0:T(2,128)(2,1)S(1)}, u32[]{:S(2)}, u32[]{:S(2)}) async-start(bf16[4,2,35840]{2,1,0:T(2,128)(2,1)} %reshape.67), calls=%async_computation | async-start | bytes 1146880 | tf_op jit(solution)/shard_map/all_to_all | solution.py:113
  247.4 537.6 %all-reduce.3.cloned.1.call-start = ((), (), s32[]{:S(2)}) async-start(), calls=%async_computation.4 | async-start | bytes 4587520
  705.9 1.4 copy-start
  705.9 1.4 copy-start.8
  705.9 79.2 %copy-start.3 = (bf16[2,4,14,2560]{3,1,2,0:T(4,128)(2,1)S(1)}, bf16[2,4,14,2560]{3,1,2,0:T(4,128)(2,1)}, u32[]{:S(2)}) copy-start(bf16[2,4,14,2560]{3,1,2,0:T(4,128)(2,1)} %copy-done.2) | copy-start | bytes 1720324
Sparse Core Ops, SparseCore 0:
  8.9 135.7 all-gather.3
  146.2 63.7 all-gather.5
  211.6 493.7 all-gather.7
  707.7 77.3 all-reduce.2
where the time goes:
time: 795 us; the launch traced here: 794 us
  waiting for transfers between devices  711 us (89%)
  local copies, waits for them, and re-layouts  44.5 us (6%)
  between operations  14 us (2%)
  matrix products  10.5 us (1%)
  starting transfers between devices  8.8 us (1%)
    all_gather x1, waiting for transfers between devices, body(): lax.all_gather(second_kernel, 'img', axis=2, tiled=True)  427 us
    all_gather x1, waiting for transfers between devices, body(): piece = lax.all_gather(first_kernel, 'img', axis=2, tiled=True)  127 us
    unnamed x5, waiting for transfers between devices  78.6 us
    all_gather x1, waiting for transfers between devices, body(): lax.all_gather(projection, 'img', axis=0, tiled=True)  53.6 us
    unnamed x21, local copies, waits for them, and re-layouts  25.4 us
  transfers between devices with their start and end apart: 8, of which 7 were waited for; matrix products, arithmetic and copies ran while one was open for 7% of the time, Pallas kernels for 0%

commit v1 on v0

--- a/solution.py
+++ b/solution.py
@@ -72,6 +72,24 @@
     second_shift,
     second_kernel,
 ):
+
+    def convert_chains(block_in, out_dim):
+        n_all = lax.psum(1, "img")
+        pile = list(map(lambda idx: (idx, (idx + 1) % n_all), range(n_all)))
+        runs = list(map(lambda idx: (idx, (idx - 1) % n_all), range(n_all)))
+        lower, outcome_arr = ([block_in], [block_in])
+        for _ in range(n_all // 2):
+            lower.append(lax.ppermute(lower[-1], perm=pile, axis_name="img"))
+        kk = 0
+        while kk < (n_all - 1) // 2:
+            outcome_arr.append(lax.ppermute(outcome_arr[-1], "img", perm=runs))
+            kk += 1
+        return jnp.roll(
+            jnp.concatenate([*lower[::-1], *outcome_arr[1:]], axis=out_dim),
+            (lax.axis_index("img") - n_all // 2) * block_in.shape[out_dim],
+            axis=out_dim,
+        )
+
     section_id = lax.axis_index("section")
     is_first = section_id == 0
     is_second = section_id == 1
@@ -106,7 +124,7 @@
         return lax.cond(is_first, project_compute, lambda: total)
 
     proj_empty = jnp.zeros((flat_pooled.shape[0], wide), jnp.float32)
-    summed_proj = project_piece(proj_empty, lax.all_gather(projection, "img", axis=0, tiled=True))
+    summed_proj = project_piece(proj_empty, convert_chains(projection, 0))
     own_rows = summed_proj.astype(jnp.bfloat16).reshape(images, out_rows, out_cols, wide)
     arrived = from_behind(own_rows, "section", 1)
     sorted_layout = arrange_groups(arrived, groups, shards)

time: 795 us -> 771 us (0.970)
  waiting for transfers between devices: 711 us -> 659 us
  local copies, waits for them, and re-layouts: 44.5 us -> 58.8 us
  starting transfers between devices: 8.8 us -> 21.2 us
    ppermute x0 -> x3, waiting for transfers between devices: none -> 86.7 us  [the longest x2 57 us: convert_chains(): lower.append(lax.ppermute(lower[-1], perm=pile, axis_name='img'))]
    all_gather x1, waiting for transfers between devices: 127 us -> 55.4 us  [body(): piece = lax.all_gather(first_kernel, 'img', axis=2, tiled=True)]
    all_gather x1 -> x0, waiting for transfers between devices: 53.6 us -> none  [body(): lax.all_gather(projection, 'img', axis=0, tiled=True)]
    ppermute x0 -> x3, starting transfers between devices: none -> 13.6 us  [the longest x2 13.5 us: convert_chains(): lower.append(lax.ppermute(lower[-1], perm=pile, axis_name='img'))]
    all_gather x1, waiting for transfers between devices: 427 us -> 414 us  [body(): lax.all_gather(second_kernel, 'img', axis=2, tiled=True)]
    unnamed x21 -> x32, local copies, waits for them, and re-layouts: 25.4 us -> 37.7 us
    unnamed x5 -> x4, waiting for transfers between devices: 78.6 us -> 77.8 us
  transfers between devices with their start and end apart: 8 -> 10, of which waited for: 7 -> 9; matrix products, arithmetic and copies ran while one was open for 7% -> 9% of each run, Pallas kernels for 0% -> 0%
where the time goes in v1:
time: 771 us; the launch traced here: 770 us
  waiting for transfers between devices  659 us (85%)
  local copies, waits for them, and re-layouts  58.8 us (8%)
  starting transfers between devices  21.2 us (3%)
  between operations  13.9 us (2%)
  matrix products  11.8 us (2%)
    all_gather x1, waiting for transfers between devices, body(): lax.all_gather(second_kernel, 'img', axis=2, tiled=True)  414 us
    unnamed x4, waiting for transfers between devices  77.8 us
    ppermute x2, waiting for transfers between devices, convert_chains(): lower.append(lax.ppermute(lower[-1], perm=pile, axis_name='img'))  57 us
    all_gather x1, waiting for transfers between devices, body(): piece = lax.all_gather(first_kernel, 'img', axis=2, tiled=True)  55.4 us
    unnamed x32, local copies, waits for them, and re-layouts  37.7 us
    ppermute x1, waiting for transfers between devices, convert_chains(): outcome_arr.append(lax.ppermute(outcome_arr[-1], 'img', perm=runs))  29.7 us
  transfers between devices with their start and end apart: 10, of which 9 were waited for; matrix products, arithmetic and copies ran while one was open for 9% of the time, Pallas kernels for 0%

profile of v1, /device:TPU:0, one launch (start us, length us, event | category | flops | bytes accessed | tf_op | source)
XLA Modules:
  0.0 770.5 jit_solution(857650705995649198)
XLA Ops:
  8.4 3.1 collective-permute-start
  11.5 27.6 %collective-permute-done = bf16[160,2560]{1,0:T(8,128)(2,1)} collective-permute-done((bf16[160,2560]{1,0:T(8,128)(2,1)S(1)}, bf16[160,2560]{1,0:T(8,128)(2,1)}, u32[]{:S(2)}, u32[]{:S(2)}) %collective-permute-start) | collective-permute-done | bytes 819232 | tf_op jit(solution)/shard_map/ppermute | solution.py:82
  39.1 10.4 %collective-permute-start.1 = (bf16[160,2560]{1,0:T(8,128)(2,1)}, bf16[160,2560]{1,0:T(8,128)(2,1)}, u32[]{:S(2)}, u32[]{:S(2)}) collective-permute-start(bf16[160,2560]{1,0:T(8,128)(2,1)} %collective-permute-done), channel_id=1, source_target_pairs={{0,4},{4,8},{8,12},{12,0},{1,5},{5,9},{9,13},{13,1},{2,6},{6,10},{... | collective-permute-start | bytes 2457608 | tf_op jit(solution)/shard_map/ppermute | solution.py:82
  52.6 3.5 collective-permute-done.4
  56.8 29.4 %collective-permute-done.1 = bf16[160,2560]{1,0:T(8,128)(2,1)} collective-permute-done((bf16[160,2560]{1,0:T(8,128)(2,1)}, bf16[160,2560]{1,0:T(8,128)(2,1)}, u32[]{:S(2)}, u32[]{:S(2)}) %collective-permute-start.1) | collective-permute-done | bytes 819232 | tf_op jit(solution)/shard_map/ppermute | solution.py:82
  91.4 29.7 %collective-permute-done.2 = bf16[160,2560]{1,0:T(8,128)(2,1)} collective-permute-done((bf16[160,2560]{1,0:T(8,128)(2,1)S(1)}, bf16[160,2560]{1,0:T(8,128)(2,1)}, u32[]{:S(2)}, u32[]{:S(2)}) %collective-permute-start.2) | collective-permute-done | bytes 819232 | tf_op jit(solution)/shard_map/ppermute | solution.py:85
  121.1 2.1 constant_dynamic-update-slice_fusion.4
  125.3 2.2 constant_dynamic-update-slice_fusion.2
  128.4 2.1 constant_dynamic-update-slice_fusion
  130.5 55.4 %all-gather.3.cloned.1.call-done = bf16[3,3,640,640]{3,2,1,0:T(8,128)(2,1)} async-done(((bf16[3,3,160,640]{3,2,1,0:T(8,128)(2,1)}), bf16[3,3,640,640]{3,2,1,0:T(8,128)(2,1)}) %all-gather.3.cloned.1.call-update) | async-done | bytes 7372816 | tf_op jit(solution)/shard_map/all_gather | solution.py:108
  186.0 9.8 %conditional.3 = (f32[2,8,28,640]{3,1,2,0:T(8,128)S(1)}) conditional(s32[]{:T(128)} %convert_element_type.60, () %tuple.38, (bf16[2,10,28,640]{3,1,2,0:T(8,128)(2,1)S(1)}, bf16[3,3,640,640]{3,2,1,0:T(8,128)(2,1)}) %tuple.39), branch_computations={%region_0.1_spmd, %region_1.2_spmd} | conditional | flops 3778887680 | bytes 21739878 | solution.py:113
  187.0 7.9 %convolution_select_fusion = f32[8,16,4,640]{3,1,2,0:T(8,128)S(1)} fusion(bf16[3,3,640,640]{3,2,1,0:T(8,128)(2,1)} %get-tuple-element.102, bf16[10,2,7,2,640]{4,2,1,3,0:T(8,128)(2,1)S(1)} %slice.12, bf16[10,2,8,4,640]{4,2,1,3,0:T(8,128)(2,1)S(1)} %copy.75, pred[16,4]{0,1:T(4,128)(4,1)S(1)} %copy-done.11), kind=kOutput, calls=%fused_computation.2 | convolution fusion | flops 3778887680 | bytes 9861184 | tf_op jit(solution)/shard_map/cond/branch_1_fun/conv_general_dilated | solution.py:33
  197.6 4.7 conditional.4
  197.7 3.9 fusion.11
  203.8 12.5 %collective-permute-done.5 = bf16[2,4,14,2560]{3,1,2,0:T(4,128)(2,1)S(1)} collective-permute-done((bf16[2,4,14,2560]{3,1,2,0:T(4,128)(2,1)S(1)}, bf16[2,4,14,2560]{3,1,2,0:T(4,128)(2,1)S(1)}, u32[]{:S(2)}, u32[]{:S(2)}) %collective-permute-start.5) | collective-permute-done | bytes 573472 | tf_op jit(solution)/shard_map/ppermute | solution.py:29
  217.3 5.7 copy.90
  223.0 10.2 %reshape.70 = bf16[4,2,35840]{2,1,0:T(2,128)(2,1)} reshape(bf16[2560,2,4,14]{3,2,1,0:T(4,128)(2,1)} %bitcast.55) | data formatting | bytes 1146880
  233.1 3.5 all-to-all-start
  237.0 8.9 %all-to-all-done = bf16[4,2,35840]{2,1,0:T(2,128)(2,1)S(1)} async-done(((bf16[4,2,35840]{2,1,0:T(2,128)(2,1)}), bf16[4,2,35840]{2,1,0:T(2,128)(2,1)S(1)}, u32[]{:S(2)}, u32[]{:S(2)}) %all-to-all-start) | async-done | bytes 573472 | tf_op jit(solution)/shard_map/all_to_all | solution.py:131
  245.9 12.7 %reshape.71 = bf16[2560,2,4,14]{3,2,1,0:T(4,128)(2,1)} reshape(bf16[4,2,35840]{2,1,0:T(2,128)(2,1)S(1)} %all-to-all-done) | data formatting | bytes 1146880
  258.7 6.8 copy.86
  267.5 414.4 %all-gather.5.cloned.1.call-done = bf16[3,3,640,2560]{3,2,1,0:T(8,128)(2,1)} async-done(((bf16[3,3,160,2560]{3,2,1,0:T(8,128)(2,1)}), bf16[3,3,640,2560]{3,2,1,0:T(8,128)(2,1)}) %all-gather.5.cloned.1.call-update) | async-done | bytes 29491216 | tf_op jit(solution)/shard_map/all_gather | solution.py:147
  684.9 76.4 %all-reduce.3.cloned.1.call-done = bf16[2,16,14,2560]{3,1,2,0:T(8,128)(2,1)} async-done(((bf16[2,16,14,2560]{3,1,2,0:T(8,128)(2,1)}), bf16[2,16,14,2560]{3,1,2,0:T(8,128)(2,1)}) %all-reduce.3.cloned.1.call-update) | async-done | bytes 2293776
  761.3 2.7 fusion.32
  (70 shorter events, 25.6 us)
Async XLA Ops:
  6.5 179.4 %all-gather.3.cloned.1.call-start = ((), (), s32[]{:S(2)}) async-start(), calls=%async_computation.1 | async-start | bytes 9216000 | tf_op jit(solution)/shard_map/all_gather | solution.py:108
  7.3 1.1 copy-start.1
  7.3 42.3 %copy-start.2 = (bf16[2,8,28,640]{3,1,2,0:T(8,128)(2,1)S(1)}, bf16[2,8,28,640]{3,1,2,0:T(8,128)(2,1)}, u32[]{:S(2)}) copy-start(bf16[2,8,28,640]{3,1,2,0:T(8,128)(2,1)} %param.14) | copy-start | bytes 1720324
  7.3 42.3 %copy-start.8 = (f32[640]{0:T(1024)S(1)}, f32[640]{0:T(1024)}, u32[]{:S(2)}) copy-start(f32[640]{0:T(1024)} %param.16) | copy-start | bytes 7684
  7.3 42.3 %copy-start.9 = (f32[640]{0:T(1024)S(1)}, f32[640]{0:T(1024)}, u32[]{:S(2)}) copy-start(f32[640]{0:T(1024)} %param.15) | copy-start | bytes 7684
  7.3 674.6 %all-gather.5.cloned.1.call-start = ((), (), s32[]{:S(2)}) async-start(), calls=%async_computation.2 | async-start | bytes 36864000 | tf_op jit(solution)/shard_map/all_gather | solution.py:147
  8.4 30.7 %collective-permute-start = (bf16[160,2560]{1,0:T(8,128)(2,1)S(1)}, bf16[160,2560]{1,0:T(8,128)(2,1)}, u32[]{:S(2)}, u32[]{:S(2)}) collective-permute-start(bf16[160,2560]{1,0:T(8,128)(2,1)S(1)} %copy-done.1), channel_id=1, source_target_pairs={{0,4},{4,8},{8,12},{12,0},{1,5},{5,9},{9,13},{13,1},{2,6},{6,10},{... | collective-permute-start | bytes 2457608 | tf_op jit(solution)/shard_map/ppermute | solution.py:82
  39.1 47.1 %collective-permute-start.1 = (bf16[160,2560]{1,0:T(8,128)(2,1)}, bf16[160,2560]{1,0:T(8,128)(2,1)}, u32[]{:S(2)}, u32[]{:S(2)}) collective-permute-start(bf16[160,2560]{1,0:T(8,128)(2,1)} %collective-permute-done), channel_id=1, source_target_pairs={{0,4},{4,8},{8,12},{12,0},{1,5},{5,9},{9,13},{13,1},{2,6},{6,10},{... | collective-permute-start | bytes 2457608 | tf_op jit(solution)/shard_map/ppermute | solution.py:82
  49.9 2.7 collective-permute-start.3
  51.2 4.9 collective-permute-start.4
  52.5 68.6 %collective-permute-start.2 = (bf16[160,2560]{1,0:T(8,128)(2,1)S(1)}, bf16[160,2560]{1,0:T(8,128)(2,1)}, u32[]{:S(2)}, u32[]{:S(2)}) collective-permute-start(bf16[160,2560]{1,0:T(8,128)(2,1)S(1)} %copy-done.1), channel_id=1, source_target_pairs={{0,12},{4,0},{8,4},{12,8},{1,13},{5,1},{9,5},{13,9},{2,14},{6,2},{... | collective-permute-start | bytes 2457608 | tf_op jit(solution)/shard_map/ppermute | solution.py:85
  186.0 9.8 %copy-start.3 = (bf16[2,8,28,640]{3,1,2,0:T(8,128)(2,1)S(1)}, bf16[2,8,28,640]{3,1,2,0:T(8,128)(2,1)}, u32[]{:S(2)}) copy-start(bf16[2,8,28,640]{3,1,2,0:T(8,128)(2,1)} %param.14) | copy-start | bytes 1720324
  186.4 0.7 copy-start.11
  202.2 20.7 %copy-start.4 = (bf16[2,4,14,2560]{3,1,2,0:T(4,128)(2,1)}, bf16[2,4,14,2560]{3,1,2,0:T(4,128)(2,1)S(1)}, u32[]{:S(2)}) copy-start(bf16[2,4,14,2560]{3,1,2,0:T(4,128)(2,1)S(1)} %get-tuple-element.138) | copy-start | bytes 1720324
  202.3 14.0 %collective-permute-start.5 = (bf16[2,4,14,2560]{3,1,2,0:T(4,128)(2,1)S(1)}, bf16[2,4,14,2560]{3,1,2,0:T(4,128)(2,1)S(1)}, u32[]{:S(2)}, u32[]{:S(2)}) collective-permute-start(bf16[2,4,14,2560]{3,1,2,0:T(4,128)(2,1)S(1)} %get-tuple-element.138), channel_id=1, source_target_pairs={{0,16},{1,17},{2,18},{3,19},{4,20},{5,21},{6,22},{7,23},{8,24},{9,... | collective-permute-start | bytes 1720328 | tf_op jit(solution)/shard_map/ppermute | solution.py:29
  223.0 13.7 %copy-start.6 = (f32[2560]{0:T(1024)S(1)}, f32[2560]{0:T(1024)}, u32[]{:S(2)}) copy-start(f32[2560]{0:T(1024)} %param.19) | copy-start | bytes 30724
  223.0 13.8 %copy-start.7 = (f32[2560]{0:T(1024)S(1)}, f32[2560]{0:T(1024)}, u32[]{:S(2)}) copy-start(f32[2560]{0:T(1024)} %param.20) | copy-start | bytes 30724
  233.1 12.8 %all-to-all-start = ((bf16[4,2,35840]{2,1,0:T(2,128)(2,1)}), bf16[4,2,35840]{2,1,0:T(2,128)(2,1)S(1)}, u32[]{:S(2)}, u32[]{:S(2)}) async-start(bf16[4,2,35840]{2,1,0:T(2,128)(2,1)} %reshape.70), calls=%async_computation | async-start | bytes 1146880 | tf_op jit(solution)/shard_map/all_to_all | solution.py:131
  236.6 524.7 %all-reduce.3.cloned.1.call-start = ((), (), s32[]{:S(2)}) async-start(), calls=%async_computation.3 | async-start | bytes 4587520
  682.4 1.4 copy-start
  682.4 1.4 copy-start.10
  682.4 78.9 %copy-start.5 = (bf16[2,4,14,2560]{3,1,2,0:T(4,128)(2,1)S(1)}, bf16[2,4,14,2560]{3,1,2,0:T(4,128)(2,1)}, u32[]{:S(2)}) copy-start(bf16[2,4,14,2560]{3,1,2,0:T(4,128)(2,1)} %copy-done.4) | copy-start | bytes 1720324
Sparse Core Ops, SparseCore 0:
  8.9 177.0 all-gather.2
  187.6 494.2 all-gather.4
  684.3 76.9 all-reduce.2
